TPU v7x, 32 devices: a whole 2x2x4 slice. The times are simulated.
32 devices in a mesh: gy: 4 (over y, x), gz: 8 (over z, core).
Axes of the slice: x: 2, y: 2, z: 4, core: 2. Of those that a mesh axis runs over, the one named last changes fastest.
Arguments:
- conduct: float32 [64, 256, 128], P('gy', 'gz'), may hold values from 0.3 to 3
- seeds: int32 [64, 256, 128], P('gy', 'gz'), may hold values 0 or 1
- labels: int32 [64, 256, 128], P('gy', 'gz'), may hold values 0 or 1
- start: float32 [64, 256, 128], P('gy', 'gz'), may hold values from 0 to 1
- cotangent: float32 [64, 256, 128], P('gy', 'gz'), may hold values from -12 to 12
Outputs:
- probability: float32 [64, 256, 128], P('gy', 'gz')
- adjoint: float32 [64, 256, 128], P('gy', 'gz')
- grad_conduct: float32 [64, 256, 128], P('gy', 'gz')
All inputs are finite; a program needn't handle non-finite values. No bound on the sum of `seeds` or of `labels` on one device may be relied on, other than what follows from the above.
Results may differ from a plain program's by a relative error of at most 0.0001.
Values sent between devices are 32-bit elements; how exact they have to be, the bound alone decides.
A program may use at most 64 MiB of HBM per device.

v0:
```python
import jax
import jax.numpy as jnp
from jax import lax
from jax.sharding import PartitionSpec as P

ITERS = 2


seed_pull = 4.0
screening = 0.05


def with_halo(block, sides, width):
    for axis, dim in sides:
        count = lax.axis_size(axis)
        forward = [(i, i + 1) for i in range(count - 1)]
        backward = [(target, source) for source, target in forward]
        low = lax.ppermute(
            lax.slice_in_dim(block, block.shape[dim] - width, None, axis=dim), axis, forward
        )
        high = lax.ppermute(lax.slice_in_dim(block, 0, width, axis=dim), axis, backward)
        block = jnp.concatenate([low, block, high], axis=dim)
    return block


def harmonic(first, second):
    return 2.0 * first * second / (first + second)


def faces(field):
    return with_halo(field, (("gy", 0), ("gz", 1)), 1)


def coefficients(padded_cond, seeds):
    core = padded_cond[1:-1, 1:-1]
    along = jnp.pad(core, ((0, 0), (0, 0), (1, 1)))
    weights = (
        harmonic(core, padded_cond[2:, 1:-1]),
        harmonic(core, padded_cond[:-2, 1:-1]),
        harmonic(core, padded_cond[1:-1, 2:]),
        harmonic(core, padded_cond[1:-1, :-2]),
        harmonic(core, along[..., 2:]),
        harmonic(core, along[..., :-2]),
    )
    diagonal = weights[0] + weights[1] + weights[2] + weights[3] + weights[4] + weights[5]
    diagonal = diagonal + seed_pull * seeds.astype(jnp.float32) + screening
    return (diagonal,) + weights


def operate(padded, coeffs):
    field = padded[1:-1, 1:-1]
    along = jnp.pad(field, ((0, 0), (0, 0), (1, 1)))
    out = coeffs[0] * field - coeffs[1] * padded[2:, 1:-1] - coeffs[2] * padded[:-2, 1:-1]
    out = out - coeffs[3] * padded[1:-1, 2:] - coeffs[4] * padded[1:-1, :-2]
    return out - coeffs[5] * along[..., 2:] - coeffs[6] * along[..., :-2]


def edge_term(ci, cj, ui, uj, vi, vj):
    total = ci + cj
    return -2.0 * cj * cj / (total * total) * (ui - uj) * (vi - vj)


def gradient(cond_pad, prob_pad, adj_pad):
    ci = cond_pad[1:-1, 1:-1]
    ui = prob_pad[1:-1, 1:-1]
    vi = adj_pad[1:-1, 1:-1]
    out = edge_term(ci, cond_pad[2:, 1:-1], ui, prob_pad[2:, 1:-1], vi, adj_pad[2:, 1:-1])
    out = out + edge_term(ci, cond_pad[:-2, 1:-1], ui, prob_pad[:-2, 1:-1], vi, adj_pad[:-2, 1:-1])
    out = out + edge_term(ci, cond_pad[1:-1, 2:], ui, prob_pad[1:-1, 2:], vi, adj_pad[1:-1, 2:])
    out = out + edge_term(ci, cond_pad[1:-1, :-2], ui, prob_pad[1:-1, :-2], vi, adj_pad[1:-1, :-2])
    cx = jnp.pad(ci, ((0, 0), (0, 0), (1, 1)))
    ux = jnp.pad(ui, ((0, 0), (0, 0), (1, 1)))
    vx = jnp.pad(vi, ((0, 0), (0, 0), (1, 1)))
    out = out + edge_term(ci, cx[..., 2:], ui, ux[..., 2:], vi, vx[..., 2:])
    return out + edge_term(ci, cx[..., :-2], ui, ux[..., :-2], vi, vx[..., :-2])


def paired_sums(resid, image):
    return lax.psum((jnp.sum(resid * resid), jnp.sum(resid * image)), ("gy", "gz"))


def conjugate(iterate, iterate_pad, resid, coeffs):
    resid_pad = faces(resid)
    image = operate(resid_pad, coeffs)
    norm_now, product = paired_sums(resid, image)
    alpha = norm_now / product
    direction, direction_pad, along = (resid, resid_pad, image)
    for step in range(ITERS):
        iterate = iterate + alpha * direction
        resid = resid - alpha * along
        if step + 1 < ITERS:
            resid_pad = faces(resid)
            image = operate(resid_pad, coeffs)
            norm_next, product = paired_sums(resid, image)
            ratio = norm_next / norm_now
            alpha = norm_next / (product - ratio * norm_next / alpha)
            direction = resid + ratio * direction
            along = image + ratio * along
            norm_now = norm_next
    return (iterate, iterate_pad)


def per_device(conduct, seeds, labels, start, cotangent):
    cond_pad = with_halo(conduct, (("gy", 0), ("gz", 1)), 1)
    start_pad = faces(start)
    coeffs = coefficients(cond_pad, seeds)
    rhs = seed_pull * (seeds * labels).astype(jnp.float32)
    first_resid = rhs - operate(start_pad, coeffs)
    probability, prob_pad = conjugate(start, start_pad, first_resid, coeffs)
    adjoint, adj_pad = conjugate(
        jnp.zeros_like(cotangent), jnp.zeros_like(start_pad), cotangent, coeffs
    )
    paired = with_halo(jnp.stack([probability, adjoint]), (("gy", 1), ("gz", 2)), 1)
    prob_pad = paired[0]
    adj_pad = paired[1]
    grad_conduct = gradient(cond_pad, prob_pad, adj_pad)
    return (probability, adjoint, grad_conduct)


def solution(mesh):
    in_specs = (
        P("gy", "gz", None),
        P("gy", "gz", None),
        P("gy", "gz", None),
        P("gy", "gz", None),
        P("gy", "gz", None),
    )
    out_specs = (P("gy", "gz", None), P("gy", "gz", None), P("gy", "gz", None))
    return jax.shard_map(
        per_device, mesh=mesh, in_specs=in_specs, out_specs=out_specs, check_vma=False
    )
```

profile of v0, /device:TPU:0, one launch (start us, length us, event | category | flops | bytes accessed | tf_op | source)
XLA Modules:
  0.0 200.8 jit_solution(3476084306509242845)
XLA Ops:
  0.6 0.7 fusion.110
  1.4 1.3 collective-permute-start.4
  2.7 5.5 %collective-permute-start.5 = (f32[1,32,128]{2,1,0:T(8,128)S(1)}, f32[1,32,128]{2,1,0:T(8,128)S(1)}, u32[]{:S(2)}, u32[]{:S(2)}) collective-permute-start(f32[1,32,128]{2,1,0:T(8,128)S(1)} %get-tuple-element.50), channel_id=1, source_target_pairs={{0,8},{8,16},{16,24},{1,9},{9,17},{17,25},{2,10},{10,18},{18,26},{... | collective-permute-start | bytes 49160 | tf_op jit(solution)/shard_map/ppermute | solution.py:18
  8.2 0.7 fusion.111
  8.9 4.8 %collective-permute-start.1 = (f32[1,32,128]{2,1,0:T(8,128)S(1)}, f32[1,32,128]{2,1,0:T(8,128)S(1)}, u32[]{:S(2)}, u32[]{:S(2)}) collective-permute-start(f32[1,32,128]{2,1,0:T(8,128)S(1)} %get-tuple-element.52), channel_id=1, source_target_pairs={{0,8},{8,16},{16,24},{1,9},{9,17},{17,25},{2,10},{10,18},{18,26},{... | collective-permute-start | bytes 49160 | tf_op jit(solution)/shard_map/ppermute | solution.py:18
  13.7 0.7 fusion.112
  14.5 1.3 collective-permute-start.16
  15.8 4.5 %collective-permute-start.17 = (f32[1,32,128]{2,1,0:T(8,128)S(1)}, f32[1,32,128]{2,1,0:T(8,128)S(1)}, u32[]{:S(2)}, u32[]{:S(2)}) collective-permute-start(f32[1,32,128]{2,1,0:T(8,128)S(1)} %get-tuple-element.54), channel_id=1, source_target_pairs={{0,8},{8,16},{16,24},{1,9},{9,17},{17,25},{2,10},{10,18},{18,26},{... | collective-permute-start | bytes 49160 | tf_op jit(solution)/shard_map/ppermute | solution.py:18
  20.3 1.3 collective-permute-start
  21.6 1.0 constant_dynamic-update-slice_fusion.1
  22.7 3.3 %collective-permute-done = f32[1,32,128]{2,1,0:T(8,128)S(1)} collective-permute-done((f32[1,32,128]{2,1,0:T(8,128)S(1)}, f32[1,32,128]{2,1,0:T(8,128)S(1)}, u32[]{:S(2)}, u32[]{:S(2)}) %collective-permute-start) | collective-permute-done | bytes 16416 | tf_op jit(solution)/shard_map/ppermute | solution.py:21
  26.0 1.3 collective-permute-start.3
  27.3 1.3 collective-permute-start.2
  28.7 1.3 collective-permute-start.18
  30.0 5.5 %collective-permute-start.19 = (f32[18,1,128]{2,1,0:T(1,128)S(1)}, f32[18,1,128]{2,1,0:T(1,128)S(1)}, u32[]{:S(2)}, u32[]{:S(2)}) collective-permute-start(f32[18,1,128]{2,1,0:T(1,128)S(1)} %get-tuple-element.42), channel_id=1, source_target_pairs={{0,1},{1,2},{2,3},{3,4},{4,5},{5,6},{6,7},{8,9},{9,10},{10,11},{11... | collective-permute-start | bytes 27656 | tf_op jit(solution)/shard_map/ppermute | solution.py:18
  35.6 1.4 collective-permute-start.6
  37.0 4.4 %collective-permute-start.7 = (f32[18,1,128]{2,1,0:T(1,128)S(1)}, f32[18,1,128]{2,1,0:T(1,128)S(1)}, u32[]{:S(2)}, u32[]{:S(2)}) collective-permute-start(f32[18,1,128]{2,1,0:T(1,128)S(1)} %get-tuple-element.38), channel_id=1, source_target_pairs={{0,1},{1,2},{2,3},{3,4},{4,5},{5,6},{6,7},{8,9},{9,10},{10,11},{11... | collective-permute-start | bytes 27656 | tf_op jit(solution)/shard_map/ppermute | solution.py:18
  41.5 1.2 multiply_reduce_fusion.1
  43.2 4.3 %collective-permute-start.9 = (f32[1,32,128]{2,1,0:T(8,128)S(1)}, f32[1,32,128]{2,1,0:T(8,128)S(1)}, u32[]{:S(2)}, u32[]{:S(2)}) collective-permute-start(f32[1,32,128]{2,1,0:T(8,128)S(1)} %get-tuple-element.47), channel_id=1, source_target_pairs={{0,8},{8,16},{16,24},{1,9},{9,17},{17,25},{2,10},{10,18},{18,26},{... | collective-permute-start | bytes 49160 | tf_op jit(solution)/shard_map/ppermute | solution.py:18
  47.5 1.3 collective-permute-start.8
  48.9 4.2 %collective-permute-done.8 = f32[1,32,128]{2,1,0:T(8,128)S(1)} collective-permute-done((f32[1,32,128]{2,1,0:T(8,128)S(1)}, f32[1,32,128]{2,1,0:T(8,128)S(1)}, u32[]{:S(2)}, u32[]{:S(2)}) %collective-permute-start.8) | collective-permute-done | bytes 16416 | tf_op jit(solution)/shard_map/ppermute | solution.py:21
  53.1 1.3 collective-permute-start.10
  54.4 3.0 %collective-permute-start.11 = (f32[18,1,128]{2,1,0:T(1,128)S(1)}, f32[18,1,128]{2,1,0:T(1,128)S(1)}, u32[]{:S(2)}, u32[]{:S(2)}) collective-permute-start(f32[18,1,128]{2,1,0:T(1,128)S(1)} %get-tuple-element.36), channel_id=1, source_target_pairs={{0,1},{1,2},{2,3},{3,4},{4,5},{5,6},{6,7},{8,9},{9,10},{10,11},{11... | collective-permute-start | bytes 27656 | tf_op jit(solution)/shard_map/ppermute | solution.py:18
  57.5 0.8 collective-permute-done.11
  58.3 1.0 multiply_reduce_fusion.4
  59.3 43.4 %all-reduce.9 = (f32[]{:T(128)}, f32[]{:T(128)}, f32[]{:T(128)}, f32[]{:T(128)}) all-reduce(f32[]{:T(128)} %get-tuple-element.6, f32[]{:T(128)} %get-tuple-element.5, f32[]{:T(128)} %get-tuple-element.4, f32[]{:T(128)} %get-tuple-element.3), channel_id=1, replica_groups=mesh['gy'=4,'gz'=8] {'gy','gz'}, use_global_device_ids=true, to_apply=%region_1.2 | all-reduce | flops 4 | bytes 32 | tf_op jit(solution)/shard_map/psum | solution.py:79
  104.1 0.7 multiply_reduce_fusion
  104.8 0.6 fusion.107
  105.4 4.2 %collective-permute-start.21 = (f32[1,32,128]{2,1,0:T(8,128)}, f32[1,32,128]{2,1,0:T(8,128)S(1)}, u32[]{:S(2)}, u32[]{:S(2)}) collective-permute-start(f32[1,32,128]{2,1,0:T(8,128)} %get-tuple-element.43), channel_id=1, source_target_pairs={{0,8},{8,16},{16,24},{1,9},{9,17},{17,25},{2,10},{10,18},{18,26},{... | collective-permute-start | bytes 49160 | tf_op jit(solution)/shard_map/ppermute | solution.py:18
  109.6 1.3 collective-permute-start.20
  112.3 0.7 multiply_reduce_fusion.3
  113.0 4.5 %collective-permute-start.13 = (f32[1,32,128]{2,1,0:T(8,128)S(1)}, f32[1,32,128]{2,1,0:T(8,128)S(1)}, u32[]{:S(2)}, u32[]{:S(2)}) collective-permute-start(f32[1,32,128]{2,1,0:T(8,128)S(1)} %get-tuple-element.45), channel_id=1, source_target_pairs={{0,8},{8,16},{16,24},{1,9},{9,17},{17,25},{2,10},{10,18},{18,26},{... | collective-permute-start | bytes 49160 | tf_op jit(solution)/shard_map/ppermute | solution.py:18
  117.5 1.3 collective-permute-start.12
  118.8 1.3 collective-permute-start.22
  120.1 3.0 %collective-permute-start.23 = (f32[18,1,128]{2,1,0:T(1,128)S(1)}, f32[18,1,128]{2,1,0:T(1,128)S(1)}, u32[]{:S(2)}, u32[]{:S(2)}) collective-permute-start(f32[18,1,128]{2,1,0:T(1,128)S(1)} %get-tuple-element.32), channel_id=1, source_target_pairs={{0,1},{1,2},{2,3},{3,4},{4,5},{5,6},{6,7},{8,9},{9,10},{10,11},{11... | collective-permute-start | bytes 27656 | tf_op jit(solution)/shard_map/ppermute | solution.py:18
  123.2 0.5 collective-permute-done.12
  123.8 1.3 collective-permute-start.14
  125.1 3.1 %collective-permute-start.15 = (f32[18,1,128]{2,1,0:T(1,128)S(1)}, f32[18,1,128]{2,1,0:T(1,128)S(1)}, u32[]{:S(2)}, u32[]{:S(2)}) collective-permute-start(f32[18,1,128]{2,1,0:T(1,128)S(1)} %get-tuple-element.34), channel_id=1, source_target_pairs={{0,1},{1,2},{2,3},{3,4},{4,5},{5,6},{6,7},{8,9},{9,10},{10,11},{11... | collective-permute-start | bytes 27656 | tf_op jit(solution)/shard_map/ppermute | solution.py:18
  128.2 1.0 fusion.46
  129.3 1.0 fusion.36
  130.2 44.4 %all-reduce.8 = (f32[]{:T(128)}, f32[]{:T(128)}, f32[]{:T(128)}, f32[]{:T(128)}) all-reduce(f32[]{:T(128)} %get-tuple-element.17, f32[]{:T(128)} %fusion.36, f32[]{:T(128)} %get-tuple-element.15, f32[]{:T(128)} %fusion.46), channel_id=1, replica_groups=mesh['gy'=4,'gz'=8] {'gy','gz'}, use_global_device_ids=true, to_apply=%region_5.6 | all-reduce | flops 4 | bytes 32 | tf_op jit(solution)/shard_map/psum | solution.py:79
  184.1 4.2 %collective-permute-start.24 = (f32[2,1,32,128]{3,2,1,0:T(8,128)S(1)}, f32[2,1,32,128]{3,2,1,0:T(8,128)S(1)}, u32[]{:S(2)}, u32[]{:S(2)}) collective-permute-start(f32[2,1,32,128]{3,2,1,0:T(8,128)S(1)} %get-tuple-element.29), channel_id=1, source_target_pairs={{0,8},{8,16},{16,24},{1,9},{9,17},{17,25},{2,10},{10,18},{18,26},{... | collective-permute-start | bytes 98312 | tf_op jit(solution)/shard_map/ppermute | solution.py:18
  188.2 1.3 collective-permute-start.25
  189.8 4.2 %collective-permute-done.25 = f32[2,1,32,128]{3,2,1,0:T(8,128)S(1)} collective-permute-done((f32[2,1,32,128]{3,2,1,0:T(8,128)S(1)}, f32[2,1,32,128]{3,2,1,0:T(8,128)S(1)}, u32[]{:S(2)}, u32[]{:S(2)}) %collective-permute-start.25) | collective-permute-done | bytes 32800 | tf_op jit(solution)/shard_map/ppermute | solution.py:21
  194.1 1.3 collective-permute-start.26
  195.4 1.3 collective-permute-start.27
  196.7 2.5 %collective-permute-done.27 = f32[2,18,1,128]{3,2,1,0:T(1,128)S(1)} collective-permute-done((f32[2,18,1,128]{3,2,1,0:T(1,128)S(1)}, f32[2,18,1,128]{3,2,1,0:T(1,128)S(1)}, u32[]{:S(2)}, u32[]{:S(2)}) %collective-permute-start.27) | collective-permute-done | bytes 18464 | tf_op jit(solution)/shard_map/ppermute | solution.py:21
  199.4 1.4 fusion.7
  (60 shorter events, 1.4 us)
Async XLA Ops:
  1.4 34.2 %collective-permute-start.4 = (f32[1,32,128]{2,1,0:T(8,128)S(1)}, f32[1,32,128]{2,1,0:T(8,128)S(1)}, u32[]{:S(2)}, u32[]{:S(2)}) collective-permute-start(f32[1,32,128]{2,1,0:T(8,128)S(1)} %get-tuple-element.49), channel_id=1, source_target_pairs={{8,0},{16,8},{24,16},{9,1},{17,9},{25,17},{10,2},{18,10},{26,18},{... | collective-permute-start | bytes 49160 | tf_op jit(solution)/shard_map/ppermute | solution.py:21
  2.7 27.3 %collective-permute-start.5 = (f32[1,32,128]{2,1,0:T(8,128)S(1)}, f32[1,32,128]{2,1,0:T(8,128)S(1)}, u32[]{:S(2)}, u32[]{:S(2)}) collective-permute-start(f32[1,32,128]{2,1,0:T(8,128)S(1)} %get-tuple-element.50), channel_id=1, source_target_pairs={{0,8},{8,16},{16,24},{1,9},{9,17},{17,25},{2,10},{10,18},{18,26},{... | collective-permute-start | bytes 49160 | tf_op jit(solution)/shard_map/ppermute | solution.py:18
  8.9 11.4 %collective-permute-start.1 = (f32[1,32,128]{2,1,0:T(8,128)S(1)}, f32[1,32,128]{2,1,0:T(8,128)S(1)}, u32[]{:S(2)}, u32[]{:S(2)}) collective-permute-start(f32[1,32,128]{2,1,0:T(8,128)S(1)} %get-tuple-element.52), channel_id=1, source_target_pairs={{0,8},{8,16},{16,24},{1,9},{9,17},{17,25},{2,10},{10,18},{18,26},{... | collective-permute-start | bytes 49160 | tf_op jit(solution)/shard_map/ppermute | solution.py:18
  14.5 14.2 %collective-permute-start.16 = (f32[1,32,128]{2,1,0:T(8,128)S(1)}, f32[1,32,128]{2,1,0:T(8,128)S(1)}, u32[]{:S(2)}, u32[]{:S(2)}) collective-permute-start(f32[1,32,128]{2,1,0:T(8,128)S(1)} %get-tuple-element.53), channel_id=1, source_target_pairs={{8,0},{16,8},{24,16},{9,1},{17,9},{25,17},{10,2},{18,10},{26,18},{... | collective-permute-start | bytes 49160 | tf_op jit(solution)/shard_map/ppermute | solution.py:21
  15.8 11.5 %collective-permute-start.17 = (f32[1,32,128]{2,1,0:T(8,128)S(1)}, f32[1,32,128]{2,1,0:T(8,128)S(1)}, u32[]{:S(2)}, u32[]{:S(2)}) collective-permute-start(f32[1,32,128]{2,1,0:T(8,128)S(1)} %get-tuple-element.54), channel_id=1, source_target_pairs={{0,8},{8,16},{16,24},{1,9},{9,17},{17,25},{2,10},{10,18},{18,26},{... | collective-permute-start | bytes 49160 | tf_op jit(solution)/shard_map/ppermute | solution.py:18
  20.3 5.6 %collective-permute-start = (f32[1,32,128]{2,1,0:T(8,128)S(1)}, f32[1,32,128]{2,1,0:T(8,128)S(1)}, u32[]{:S(2)}, u32[]{:S(2)}) collective-permute-start(f32[1,32,128]{2,1,0:T(8,128)S(1)} %get-tuple-element.51), channel_id=1, source_target_pairs={{8,0},{16,8},{24,16},{9,1},{17,9},{25,17},{10,2},{18,10},{26,18},{... | collective-permute-start | bytes 49160 | tf_op jit(solution)/shard_map/ppermute | solution.py:21
  21.6 7.0 %copy-start.2 = (f32[16,32,128]{2,1,0:T(8,128)S(1)}, f32[16,32,128]{2,1,0:T(8,128)}, u32[]{:S(2)}) copy-start(f32[16,32,128]{2,1,0:T(8,128)} %param.9) | copy-start | bytes 786436
  26.0 11.1 %collective-permute-start.3 = (f32[18,1,128]{2,1,0:T(1,128)S(1)}, f32[18,1,128]{2,1,0:T(1,128)S(1)}, u32[]{:S(2)}, u32[]{:S(2)}) collective-permute-start(f32[18,1,128]{2,1,0:T(1,128)S(1)} %get-tuple-element.39), channel_id=1, source_target_pairs={{0,1},{1,2},{2,3},{3,4},{4,5},{5,6},{6,7},{8,9},{9,10},{10,11},{11... | collective-permute-start | bytes 27656 | tf_op jit(solution)/shard_map/ppermute | solution.py:18
  27.3 14.2 %collective-permute-start.2 = (f32[18,1,128]{2,1,0:T(1,128)S(1)}, f32[18,1,128]{2,1,0:T(1,128)S(1)}, u32[]{:S(2)}, u32[]{:S(2)}) collective-permute-start(f32[18,1,128]{2,1,0:T(1,128)S(1)} %get-tuple-element.40), channel_id=1, source_target_pairs={{1,0},{2,1},{3,2},{4,3},{5,4},{6,5},{7,6},{9,8},{10,9},{11,10},{12... | collective-permute-start | bytes 27656 | tf_op jit(solution)/shard_map/ppermute | solution.py:21
  28.6 6.9 %copy-start.5 = (f32[16,32,128]{2,1,0:T(8,128)S(1)}, f32[16,32,128]{2,1,0:T(8,128)}, u32[]{:S(2)}) copy-start(f32[16,32,128]{2,1,0:T(8,128)} %param.8) | copy-start | bytes 786436
  28.7 12.8 %collective-permute-start.18 = (f32[18,1,128]{2,1,0:T(1,128)S(1)}, f32[18,1,128]{2,1,0:T(1,128)S(1)}, u32[]{:S(2)}, u32[]{:S(2)}) collective-permute-start(f32[18,1,128]{2,1,0:T(1,128)S(1)} %get-tuple-element.41), channel_id=1, source_target_pairs={{1,0},{2,1},{3,2},{4,3},{5,4},{6,5},{7,6},{9,8},{10,9},{11,10},{12... | collective-permute-start | bytes 27656 | tf_op jit(solution)/shard_map/ppermute | solution.py:21
  30.0 11.5 %collective-permute-start.19 = (f32[18,1,128]{2,1,0:T(1,128)S(1)}, f32[18,1,128]{2,1,0:T(1,128)S(1)}, u32[]{:S(2)}, u32[]{:S(2)}) collective-permute-start(f32[18,1,128]{2,1,0:T(1,128)S(1)} %get-tuple-element.42), channel_id=1, source_target_pairs={{0,1},{1,2},{2,3},{3,4},{4,5},{5,6},{6,7},{8,9},{9,10},{10,11},{11... | collective-permute-start | bytes 27656 | tf_op jit(solution)/shard_map/ppermute | solution.py:18
  35.5 6.0 %copy-start = (f32[16,32,128]{2,1,0:T(8,128)S(1)}, f32[16,32,128]{2,1,0:T(8,128)}, u32[]{:S(2)}) copy-start(f32[16,32,128]{2,1,0:T(8,128)} %param.5) | copy-start | bytes 786436
  35.5 6.0 %copy-start.1 = (s32[16,32,128]{2,1,0:T(8,128)S(1)}, s32[16,32,128]{2,1,0:T(8,128)}, u32[]{:S(2)}) copy-start(s32[16,32,128]{2,1,0:T(8,128)} %param.6) | copy-start | bytes 786436
  35.6 7.2 %collective-permute-start.6 = (f32[18,1,128]{2,1,0:T(1,128)S(1)}, f32[18,1,128]{2,1,0:T(1,128)S(1)}, u32[]{:S(2)}, u32[]{:S(2)}) collective-permute-start(f32[18,1,128]{2,1,0:T(1,128)S(1)} %get-tuple-element.37), channel_id=1, source_target_pairs={{1,0},{2,1},{3,2},{4,3},{5,4},{6,5},{7,6},{9,8},{10,9},{11,10},{12... | collective-permute-start | bytes 27656 | tf_op jit(solution)/shard_map/ppermute | solution.py:21
  37.0 5.7 %copy-start.6 = (s32[16,32,128]{2,1,0:T(8,128)S(1)}, s32[16,32,128]{2,1,0:T(8,128)}, u32[]{:S(2)}) copy-start(s32[16,32,128]{2,1,0:T(8,128)} %param.7) | copy-start | bytes 786436
  37.0 5.7 %collective-permute-start.7 = (f32[18,1,128]{2,1,0:T(1,128)S(1)}, f32[18,1,128]{2,1,0:T(1,128)S(1)}, u32[]{:S(2)}, u32[]{:S(2)}) collective-permute-start(f32[18,1,128]{2,1,0:T(1,128)S(1)} %get-tuple-element.38), channel_id=1, source_target_pairs={{0,1},{1,2},{2,3},{3,4},{4,5},{5,6},{6,7},{8,9},{9,10},{10,11},{11... | collective-permute-start | bytes 27656 | tf_op jit(solution)/shard_map/ppermute | solution.py:18
  43.2 5.7 %collective-permute-start.9 = (f32[1,32,128]{2,1,0:T(8,128)S(1)}, f32[1,32,128]{2,1,0:T(8,128)S(1)}, u32[]{:S(2)}, u32[]{:S(2)}) collective-permute-start(f32[1,32,128]{2,1,0:T(8,128)S(1)} %get-tuple-element.47), channel_id=1, source_target_pairs={{0,8},{8,16},{16,24},{1,9},{9,17},{17,25},{2,10},{10,18},{18,26},{... | collective-permute-start | bytes 49160 | tf_op jit(solution)/shard_map/ppermute | solution.py:18
  47.5 5.6 %collective-permute-start.8 = (f32[1,32,128]{2,1,0:T(8,128)S(1)}, f32[1,32,128]{2,1,0:T(8,128)S(1)}, u32[]{:S(2)}, u32[]{:S(2)}) collective-permute-start(f32[1,32,128]{2,1,0:T(8,128)S(1)} %get-tuple-element.48), channel_id=1, source_target_pairs={{8,0},{16,8},{24,16},{9,1},{17,9},{25,17},{10,2},{18,10},{26,18},{... | collective-permute-start | bytes 49160 | tf_op jit(solution)/shard_map/ppermute | solution.py:21
  53.1 4.3 %collective-permute-start.10 = (f32[18,1,128]{2,1,0:T(1,128)S(1)}, f32[18,1,128]{2,1,0:T(1,128)S(1)}, u32[]{:S(2)}, u32[]{:S(2)}) collective-permute-start(f32[18,1,128]{2,1,0:T(1,128)S(1)} %get-tuple-element.35), channel_id=1, source_target_pairs={{1,0},{2,1},{3,2},{4,3},{5,4},{6,5},{7,6},{9,8},{10,9},{11,10},{12... | collective-permute-start | bytes 27656 | tf_op jit(solution)/shard_map/ppermute | solution.py:21
  54.4 3.9 %collective-permute-start.11 = (f32[18,1,128]{2,1,0:T(1,128)S(1)}, f32[18,1,128]{2,1,0:T(1,128)S(1)}, u32[]{:S(2)}, u32[]{:S(2)}) collective-permute-start(f32[18,1,128]{2,1,0:T(1,128)S(1)} %get-tuple-element.36), channel_id=1, source_target_pairs={{0,1},{1,2},{2,3},{3,4},{4,5},{5,6},{6,7},{8,9},{9,10},{10,11},{11... | collective-permute-start | bytes 27656 | tf_op jit(solution)/shard_map/ppermute | solution.py:18
  105.4 13.4 %collective-permute-start.21 = (f32[1,32,128]{2,1,0:T(8,128)}, f32[1,32,128]{2,1,0:T(8,128)S(1)}, u32[]{:S(2)}, u32[]{:S(2)}) collective-permute-start(f32[1,32,128]{2,1,0:T(8,128)} %get-tuple-element.43), channel_id=1, source_target_pairs={{0,8},{8,16},{16,24},{1,9},{9,17},{17,25},{2,10},{10,18},{18,26},{... | collective-permute-start | bytes 49160 | tf_op jit(solution)/shard_map/ppermute | solution.py:18
  109.6 9.2 %collective-permute-start.20 = (f32[1,32,128]{2,1,0:T(8,128)S(1)}, f32[1,32,128]{2,1,0:T(8,128)S(1)}, u32[]{:S(2)}, u32[]{:S(2)}) collective-permute-start(f32[1,32,128]{2,1,0:T(8,128)S(1)} %get-tuple-element.44), channel_id=1, source_target_pairs={{8,0},{16,8},{24,16},{9,1},{17,9},{25,17},{10,2},{18,10},{26,18},{... | collective-permute-start | bytes 49160 | tf_op jit(solution)/shard_map/ppermute | solution.py:21
  113.0 10.2 %collective-permute-start.13 = (f32[1,32,128]{2,1,0:T(8,128)S(1)}, f32[1,32,128]{2,1,0:T(8,128)S(1)}, u32[]{:S(2)}, u32[]{:S(2)}) collective-permute-start(f32[1,32,128]{2,1,0:T(8,128)S(1)} %get-tuple-element.45), channel_id=1, source_target_pairs={{0,8},{8,16},{16,24},{1,9},{9,17},{17,25},{2,10},{10,18},{18,26},{... | collective-permute-start | bytes 49160 | tf_op jit(solution)/shard_map/ppermute | solution.py:18
  117.5 6.2 %collective-permute-start.12 = (f32[1,32,128]{2,1,0:T(8,128)S(1)}, f32[1,32,128]{2,1,0:T(8,128)S(1)}, u32[]{:S(2)}, u32[]{:S(2)}) collective-permute-start(f32[1,32,128]{2,1,0:T(8,128)S(1)} %get-tuple-element.46), channel_id=1, source_target_pairs={{8,0},{16,8},{24,16},{9,1},{17,9},{25,17},{10,2},{18,10},{26,18},{... | collective-permute-start | bytes 49160 | tf_op jit(solution)/shard_map/ppermute | solution.py:21
  118.8 9.4 %collective-permute-start.22 = (f32[18,1,128]{2,1,0:T(1,128)S(1)}, f32[18,1,128]{2,1,0:T(1,128)S(1)}, u32[]{:S(2)}, u32[]{:S(2)}) collective-permute-start(f32[18,1,128]{2,1,0:T(1,128)S(1)} %get-tuple-element.31), channel_id=1, source_target_pairs={{1,0},{2,1},{3,2},{4,3},{5,4},{6,5},{7,6},{9,8},{10,9},{11,10},{12... | collective-permute-start | bytes 27656 | tf_op jit(solution)/shard_map/ppermute | solution.py:21
  120.1 8.1 %collective-permute-start.23 = (f32[18,1,128]{2,1,0:T(1,128)S(1)}, f32[18,1,128]{2,1,0:T(1,128)S(1)}, u32[]{:S(2)}, u32[]{:S(2)}) collective-permute-start(f32[18,1,128]{2,1,0:T(1,128)S(1)} %get-tuple-element.32), channel_id=1, source_target_pairs={{0,1},{1,2},{2,3},{3,4},{4,5},{5,6},{6,7},{8,9},{9,10},{10,11},{11... | collective-permute-start | bytes 27656 | tf_op jit(solution)/shard_map/ppermute | solution.py:18
  123.8 5.5 %collective-permute-start.14 = (f32[18,1,128]{2,1,0:T(1,128)S(1)}, f32[18,1,128]{2,1,0:T(1,128)S(1)}, u32[]{:S(2)}, u32[]{:S(2)}) collective-permute-start(f32[18,1,128]{2,1,0:T(1,128)S(1)} %get-tuple-element.33), channel_id=1, source_target_pairs={{1,0},{2,1},{3,2},{4,3},{5,4},{6,5},{7,6},{9,8},{10,9},{11,10},{12... | collective-permute-start | bytes 27656 | tf_op jit(solution)/shard_map/ppermute | solution.py:21
  125.1 4.2 %collective-permute-start.15 = (f32[18,1,128]{2,1,0:T(1,128)S(1)}, f32[18,1,128]{2,1,0:T(1,128)S(1)}, u32[]{:S(2)}, u32[]{:S(2)}) collective-permute-start(f32[18,1,128]{2,1,0:T(1,128)S(1)} %get-tuple-element.34), channel_id=1, source_target_pairs={{0,1},{1,2},{2,3},{3,4},{4,5},{5,6},{6,7},{8,9},{9,10},{10,11},{11... | collective-permute-start | bytes 27656 | tf_op jit(solution)/shard_map/ppermute | solution.py:18
  184.0 15.1 %copy-start.3 = (f32[16,32,128]{2,1,0:T(8,128)}, f32[16,32,128]{2,1,0:T(8,128)S(1)}, u32[]{:S(2)}) copy-start(f32[16,32,128]{2,1,0:T(8,128)S(1)} %get-tuple-element.55) | copy-start | bytes 786436
  184.0 15.1 %copy-start.4 = (f32[16,32,128]{2,1,0:T(8,128)}, f32[16,32,128]{2,1,0:T(8,128)S(1)}, u32[]{:S(2)}) copy-start(f32[16,32,128]{2,1,0:T(8,128)S(1)} %get-tuple-element.56) | copy-start | bytes 786436
  184.1 5.8 %collective-permute-start.24 = (f32[2,1,32,128]{3,2,1,0:T(8,128)S(1)}, f32[2,1,32,128]{3,2,1,0:T(8,128)S(1)}, u32[]{:S(2)}, u32[]{:S(2)}) collective-permute-start(f32[2,1,32,128]{3,2,1,0:T(8,128)S(1)} %get-tuple-element.29), channel_id=1, source_target_pairs={{0,8},{8,16},{16,24},{1,9},{9,17},{17,25},{2,10},{10,18},{18,26},{... | collective-permute-start | bytes 98312 | tf_op jit(solution)/shard_map/ppermute | solution.py:18
  188.2 5.8 %collective-permute-start.25 = (f32[2,1,32,128]{3,2,1,0:T(8,128)S(1)}, f32[2,1,32,128]{3,2,1,0:T(8,128)S(1)}, u32[]{:S(2)}, u32[]{:S(2)}) collective-permute-start(f32[2,1,32,128]{3,2,1,0:T(8,128)S(1)} %get-tuple-element.30), channel_id=1, source_target_pairs={{8,0},{16,8},{24,16},{9,1},{17,9},{25,17},{10,2},{18,10},{26,18},{... | collective-permute-start | bytes 98312 | tf_op jit(solution)/shard_map/ppermute | solution.py:21
  194.1 2.6 %collective-permute-start.26 = (f32[2,18,1,128]{3,2,1,0:T(1,128)S(1)}, f32[2,18,1,128]{3,2,1,0:T(1,128)S(1)}, u32[]{:S(2)}, u32[]{:S(2)}) collective-permute-start(f32[2,18,1,128]{3,2,1,0:T(1,128)S(1)} %get-tuple-element.27), channel_id=1, source_target_pairs={{0,1},{1,2},{2,3},{3,4},{4,5},{5,6},{6,7},{8,9},{9,10},{10,11},{11... | collective-permute-start | bytes 55304 | tf_op jit(solution)/shard_map/ppermute | solution.py:18
  195.4 3.8 %collective-permute-start.27 = (f32[2,18,1,128]{3,2,1,0:T(1,128)S(1)}, f32[2,18,1,128]{3,2,1,0:T(1,128)S(1)}, u32[]{:S(2)}, u32[]{:S(2)}) collective-permute-start(f32[2,18,1,128]{3,2,1,0:T(1,128)S(1)} %get-tuple-element.28), channel_id=1, source_target_pairs={{1,0},{2,1},{3,2},{4,3},{5,4},{6,5},{7,6},{9,8},{10,9},{11,10},{12... | collective-permute-start | bytes 55304 | tf_op jit(solution)/shard_map/ppermute | solution.py:21
where the time goes:
time: 205 us; the launch traced here: 201 us
  blocking collectives  87.9 us (43%)
  starting transfers between devices  71.9 us (35%)
  waiting for transfers between devices  16 us (8%)
  between operations  13.2 us (6%)
  other arithmetic  7.82 us (4%)
  local copies, waits for them, and re-layouts  4.1 us (2%)
    psum x2, blocking collectives, paired_sums(): lax.psum((jnp.sum(resid * resid), jnp.sum(resid * image)), ('gy', 'gz'))  87.9 us
    ppermute x14, starting transfers between devices, with_halo(): lax.ppermute(lax.slice_in_dim(block, block.shape[dim] - width, None, axis...  53.7 us
    ppermute x14, starting transfers between devices, with_halo(): lax.ppermute(lax.slice_in_dim(block, 0, width, axis=dim), axis, backward)  18.2 us
    ppermute x14, waiting for transfers between devices, with_halo(): lax.ppermute(lax.slice_in_dim(block, 0, width, axis=dim), axis, backward)  14.7 us
    reduce_sum x4, other arithmetic, paired_sums(): jnp.sum(resid * image)  4.26 us
  transfers between devices with their start and end apart: 28, of which 8 were waited for; matrix products, arithmetic and copies ran while one was open for 3% of the time, Pallas kernels for 0%

commit v1 on v0

v1 whole, which is shorter than its diff:
```python
import functools

import jax
import jax.numpy as jnp
from jax import lax
from jax.experimental import pallas as pl
from jax.experimental.pallas import tpu as pltpu
from jax.sharding import PartitionSpec as P

seed_pull = 4.0
screening = 0.05

MESH = pl.DeviceIdType.MESH
COND, START, COT, RES, IMG, ADJ = range(6)
LOW_Y, HIGH_Y, LOW_Z, HIGH_Z = range(4)


def kernel(
    ny, nz,
    cond_in, seeds_in, labels_in, start_in, cot_in,
    prob_out, adj_out, grad_out,
    fields, prob, adj, grad, seeds, labels,
    edge_y, edge_z, edge_x, rim_z, halo_z, face_z, gathered,
    load_sem, store_sem, send_sem, recv_sem, gsend_sem, grecv_sem,
):
    rows, cols, lanes = cond_in.shape
    n = ny * nz
    gy = lax.axis_index("gy")
    gz = lax.axis_index("gz")
    me = gy * nz + gz
    inputs = {COND: cond_in, START: start_in, COT: cot_in}

    loads = []
    body = pl.ds(1, rows)
    for i, (src, dst) in enumerate((
        (cond_in, fields.at[COND, body]),
        (start_in, fields.at[START, body]),
        (seeds_in, seeds),
        (labels_in, labels),
        (cot_in, fields.at[COT, body]),
    )):
        copy = pltpu.make_async_copy(src, dst, load_sem.at[i])
        copy.start()
        loads.append(copy)

    barrier = pltpu.get_barrier_semaphore()
    for k in range(1, n):
        peer = lax.rem(me + k, n)
        pl.semaphore_signal(
            barrier, inc=1, device_id=(peer // nz, lax.rem(peer, nz)), device_id_type=MESH
        )

    has_low_y, has_high_y = gy > 0, gy < ny - 1
    has_low_z, has_high_z = gz > 0, gz < nz - 1
    can_send = (has_low_y, has_high_y, has_low_z, has_high_z)
    can_recv = (has_high_y, has_low_y, has_high_z, has_low_z)
    target = ((gy - 1, gz), (gy + 1, gz), (gy, gz - 1), (gy, gz + 1))

    def exchange(k, side):
        if side == LOW_Y:
            src = inputs[k].at[0] if k in inputs else fields.at[k, 1]
            dst = fields.at[k, rows + 1]
        elif side == HIGH_Y:
            src = inputs[k].at[rows - 1] if k in inputs else fields.at[k, rows]
            dst = fields.at[k, 0]
        elif side == LOW_Z:
            src = face_z.at[k, 0]
            dst = halo_z.at[k, 1]
        else:
            src = face_z.at[k, 1]
            dst = halo_z.at[k, 0]
        return pltpu.make_async_remote_copy(
            src_ref=src, dst_ref=dst, send_sem=send_sem.at[k, side],
            recv_sem=recv_sem.at[k, side], device_id=target[side], device_id_type=MESH,
        )

    def send(k, sides):
        for side in sides:
            @pl.when(can_send[side])
            def _():
                exchange(k, side).start()

    def arrive(k, sides):
        for side in sides:
            @pl.when(can_recv[side])
            def _():
                exchange(k, side).wait_recv()

    every = (LOW_Y, HIGH_Y, LOW_Z, HIGH_Z)

    def put_faces(k):
        face_z[k, 0] = fields[k, 1:rows + 1, 0:1, :]
        face_z[k, 1] = fields[k, 1:rows + 1, cols - 1:cols, :]

    plane = jnp.zeros((cols, lanes), jnp.float32)
    line = jnp.zeros((rows, 1, lanes), jnp.float32)
    for k in range(6):
        @pl.when(gy == 0)
        def _():
            fields[k, 0] = plane

        @pl.when(gy == ny - 1)
        def _():
            fields[k, rows + 1] = plane

        @pl.when(gz == 0)
        def _():
            halo_z[k, 0] = line

        @pl.when(gz == nz - 1)
        def _():
            halo_z[k, 1] = line

    loads[0].wait()
    put_faces(COND)
    loads[1].wait()
    put_faces(START)
    loads[4].wait()
    put_faces(COT)
    pl.semaphore_wait(barrier, n - 1)
    send(COND, every)
    send(START, every)
    send(COT, every)

    lane = lax.broadcasted_iota(jnp.int32, (cols, lanes), 1)
    col = lax.broadcasted_iota(jnp.int32, (cols, lanes), 0)

    def low_x(value):
        return pltpu.roll(value, 1, 1)

    def high_x(value):
        return pltpu.roll(value, lanes - 1, 1)

    def low_z(value):
        return pltpu.roll(value, 1, 0)

    def high_z(value):
        return pltpu.roll(value, cols - 1, 0)

    def weigh(low, high, keep):
        inverse = 1.0 / (low + high)
        if keep is not None:
            inverse = jnp.where(keep, inverse, 0.0)
        p = low * inverse
        q = high * inverse
        return 2.0 * high * p, 2.0 * p * p, 2.0 * q * q

    def put_edge(ref, at, parts):
        for i in range(3):
            ref[(i,) + at] = parts[i]

    def edge_step(y, carry):
        c = fields[COND, y + 1]
        put_edge(edge_x, (y,), weigh(low_x(c), c, lane > 0))
        put_edge(edge_z, (y,), weigh(low_z(c), c, col > 0))

        return carry

    def edge_y_step(y, carry):
        put_edge(edge_y, (y,), weigh(fields[COND, y], fields[COND, y + 1], None))
        return carry

    lax.fori_loop(0, rows, edge_step, 0)
    lax.fori_loop(1, rows, edge_y_step, 0)
    edge_y[0, 0] = plane
    edge_y[0, rows] = plane
    loads[2].wait()
    loads[3].wait()

    def inner_plane(k, y):
        f = fields[k, y + 1]
        pull = seed_pull * seeds[y].astype(jnp.float32) + screening
        fx = edge_x[0, y] * (f - low_x(f))
        fz = edge_z[0, y] * (f - low_z(f))
        out = pull * f + (fx - high_x(fx)) + (fz - high_z(fz))
        if not (isinstance(y, int) and y == 0):
            out = out + edge_y[0, y] * (f - fields[k, y])
        if not (isinstance(y, int) and y == rows - 1):
            out = out - edge_y[0, y + 1] * (fields[k, y + 2] - f)
        return out

    def image(k, put):
        put(0, inner_plane(k, 0))

        def step(y, carry):
            put(y, inner_plane(k, y))
            return carry

        lax.fori_loop(1, rows - 1, step, 0)
        put(rows - 1, inner_plane(k, rows - 1))

    def rim(k, out, sign):
        low = rim_z[0, 0] * (fields[k, 1:rows + 1, 0:1, :] - halo_z[k, 0])
        high = rim_z[0, 1] * (fields[k, 1:rows + 1, cols - 1:cols, :] - halo_z[k, 1])
        fields[out, 1:rows + 1, 0:1, :] = fields[out, 1:rows + 1, 0:1, :] + sign * low
        fields[out, 1:rows + 1, cols - 1:cols, :] = (
            fields[out, 1:rows + 1, cols - 1:cols, :] + sign * high
        )
        low = edge_y[0, 0] * (fields[k, 1] - fields[k, 0])
        high = edge_y[0, rows] * (fields[k, rows] - fields[k, rows + 1])
        fields[out, 1] = fields[out, 1] + sign * low
        fields[out, rows] = fields[out, rows] + sign * high

    def put_residual(y, value):
        rhs = seed_pull * (seeds[y] * labels[y]).astype(jnp.float32)
        fields[RES, y + 1] = rhs - value

    def put_image(out):
        def put(y, value):
            fields[out, y + 1] = value

        return put

    image(START, put_residual)
    image(COT, put_image(ADJ))

    arrive(COND, every)
    put_edge(edge_y, (0,), weigh(fields[COND, 0], fields[COND, 1], None))
    put_edge(edge_y, (rows,), weigh(fields[COND, rows], fields[COND, rows + 1], None))
    put_edge(rim_z, (0,), weigh(halo_z[COND, 0], fields[COND, 1:rows + 1, 0:1, :], None))
    put_edge(
        rim_z, (1,), weigh(fields[COND, 1:rows + 1, cols - 1:cols, :], halo_z[COND, 1], None)
    )
    arrive(START, every)
    rim(START, RES, -1.0)
    put_faces(RES)
    send(RES, every)
    image(RES, put_image(IMG))

    arrive(COT, every)
    rim(COT, ADJ, 1.0)
    put_faces(ADJ)

    arrive(RES, every)
    rim(RES, IMG, 1.0)
    put_faces(IMG)
    send(IMG, (HIGH_Y, HIGH_Z))
    send(ADJ, (HIGH_Y, HIGH_Z))
    send(IMG, (LOW_Y, LOW_Z))
    send(ADJ, (LOW_Y, LOW_Z))

    def fold(value):
        return jnp.sum(value.reshape(cols // 8, 8, lanes), axis=0)

    zero8 = jnp.zeros((8, lanes), jnp.float32)

    def total(value):
        return jnp.sum(jnp.sum(value, axis=0, keepdims=True), axis=1, keepdims=True)

    def shift_of(k, out):
        def step(y, carry):
            norm, product = carry
            f = fields[k, y + 1]
            return norm + fold(f * f), product + fold(f * fields[out, y + 1])

        norm, product = lax.fori_loop(0, rows, step, (zero8, zero8))
        return total(product) / jnp.maximum(total(norm), 1e-30)

    def moments(k, out, shift):
        def edge_sums(weight, df, dg):
            wf = weight * df
            wg = weight * dg
            return wf * df, wf * dg, wg * dg

        def step(y, carry):
            f = fields[k, y + 1]
            g = fields[out, y + 1] - shift * f
            pull = seed_pull * seeds[y].astype(jnp.float32) + screening
            f2, fg, g2 = f * f, f * g, g * g
            sums = [pull * f2, pull * fg, pull * g2]
            for weight, lower in ((edge_x[0, y], low_x), (edge_z[0, y], low_z)):
                more = edge_sums(weight, f - lower(f), g - lower(g))
                sums = [a + b for a, b in zip(sums, more)]
            fb = fields[k, y]
            gb = fields[out, y] - shift * fb
            keep = jnp.where(y > 0, 1.0, 0.0)
            more = edge_sums(edge_y[0, y] * keep, f - fb, g - gb)
            sums = [a + b for a, b in zip(sums, more)]
            return tuple(c + fold(v) for c, v in zip(carry, [f2, fg, g2] + sums))

        first = step_first(k, out, shift, edge_sums)
        return list(lax.fori_loop(1, rows, step, first))

    def step_first(k, out, shift, edge_sums):
        f = fields[k, 1]
        g = fields[out, 1] - shift * f
        pull = seed_pull * seeds[0].astype(jnp.float32) + screening
        f2, fg, g2 = f * f, f * g, g * g
        sums = [pull * f2, pull * fg, pull * g2]
        for weight, lower in ((edge_x[0, 0], low_x), (edge_z[0, 0], low_z)):
            more = edge_sums(weight, f - lower(f), g - lower(g))
            sums = [a + b for a, b in zip(sums, more)]
        return tuple(fold(v) for v in [f2, fg, g2] + sums)

    def rim_moments(k, out, shift, sums):
        fb, fc = fields[k, 0], fields[k, 1]
        df = fc - fb
        dg = (fields[out, 1] - fields[out, 0]) - shift * df
        wf, wg = edge_y[0, 0] * df, edge_y[0, 0] * dg
        more = [fold(v) for v in (wf * df, wf * dg, wg * dg)]
        df = fields[k, 1:rows + 1, 0:1, :] - halo_z[k, 0]
        dg = (fields[out, 1:rows + 1, 0:1, :] - halo_z[out, 0]) - shift[None] * df
        wf, wg = rim_z[0, 0] * df, rim_z[0, 0] * dg
        lines = [jnp.sum(v, axis=0) for v in (wf * df, wf * dg, wg * dg)]
        ends = sums[:3]
        for a, b, c in zip(sums[3:], more, lines):
            ends.append(jnp.sum(a + b, axis=0, keepdims=True) + c)
        return [jnp.sum(v, axis=0, keepdims=True) for v in ends[:3]] + ends[3:]

    shift_r = shift_of(RES, IMG)
    sums_r = moments(RES, IMG, shift_r)
    shift_a = shift_of(COT, ADJ)
    sums_a = moments(COT, ADJ, shift_a)
    arrive(ADJ, (HIGH_Y, HIGH_Z))
    sums_a = rim_moments(COT, ADJ, shift_a, sums_a)
    arrive(IMG, (HIGH_Y, HIGH_Z))
    sums_r = rim_moments(RES, IMG, shift_r, sums_r)

    row16 = lax.broadcasted_iota(jnp.int32, (16, lanes), 0)
    lane16 = lax.broadcasted_iota(jnp.int32, (16, lanes), 1)
    stack = jnp.zeros((16, lanes), jnp.float32)
    for base, sums in ((0, sums_r), (8, sums_a)):
        for i, value in enumerate(sums):
            stack = jnp.where(row16 == base + i, value, stack)
    stack = jnp.sum(stack, axis=1, keepdims=True)
    stack = jnp.where(row16 == 6, shift_r, stack)
    stack = jnp.where(row16 == 14, shift_a, stack)
    gathered[me] = jnp.sum(jnp.where(row16 == lane16, stack, 0.0), axis=0, keepdims=True)

    def share(k, slot):
        peer = lax.rem(me + k, n)
        return pltpu.make_async_remote_copy(
            src_ref=gathered.at[slot], dst_ref=gathered.at[slot], send_sem=gsend_sem.at[k],
            recv_sem=grecv_sem.at[k], device_id=(peer // nz, lax.rem(peer, nz)),
            device_id_type=MESH,
        )

    for k in range(1, n):
        share(k, me).start()
    arrive(IMG, (LOW_Y, LOW_Z))
    arrive(ADJ, (LOW_Y, LOW_Z))
    for k in range(1, n):
        share(k, lax.rem(me + n - k, n)).wait_recv()

    g = gathered[...].reshape(n, lanes)

    def at_shift(value, i):
        return pltpu.roll(value, 6 - i, 1)

    norm = jnp.sum(at_shift(g, 0), axis=0, keepdims=True)
    energy = jnp.sum(at_shift(g, 3), axis=0, keepdims=True)
    delta = g - energy / norm
    residual = at_shift(g, 2) + delta * (2.0 * at_shift(g, 1) + delta * at_shift(g, 0))
    product = at_shift(g, 5) + delta * (2.0 * at_shift(g, 4) + delta * at_shift(g, 3))
    alpha = norm / energy
    norm_next = alpha * alpha * jnp.sum(residual, axis=0, keepdims=True)
    product = alpha * alpha * jnp.sum(product, axis=0, keepdims=True)
    ratio = norm_next / norm
    curve = product - ratio * norm_next / alpha
    alpha_next = jnp.where(curve > 0.0, norm_next / curve, 0.0)
    on_res = alpha + alpha_next * (1.0 + ratio)
    on_img = -alpha * alpha_next
    one = lax.broadcasted_iota(jnp.int32, (1, lanes), 1)

    def pick(value, i):
        return jnp.sum(jnp.where(one == i, value, 0.0), axis=1, keepdims=True)

    res_r, img_r = pick(on_res, 6), pick(on_img, 6)
    res_a, img_a = pick(on_res, 14), pick(on_img, 14)

    def final_step(y, carry):
        prob[y] = fields[START, y] + res_r * fields[RES, y] + img_r * fields[IMG, y]
        adj[y] = res_a * fields[COT, y] + img_a * fields[ADJ, y]
        return carry

    lax.fori_loop(0, rows + 2, final_step, 0)
    stores = [
        pltpu.make_async_copy(prob.at[body], prob_out, store_sem.at[0]),
        pltpu.make_async_copy(adj.at[body], adj_out, store_sem.at[1]),
    ]
    for copy in stores:
        copy.start()

    def grad_step(y, carry):
        u, v = prob[y + 1], adj[y + 1]
        d = (u - low_x(u)) * (v - low_x(v))
        out = edge_x[1, y] * d + high_x(edge_x[2, y] * d)
        d = (u - low_z(u)) * (v - low_z(v))
        out = out + edge_z[1, y] * d + high_z(edge_z[2, y] * d)
        out = out + edge_y[1, y] * ((u - prob[y]) * (v - adj[y]))
        out = out + edge_y[2, y + 1] * ((u - prob[y + 2]) * (v - adj[y + 2]))
        grad[y] = -out
        return carry

    lax.fori_loop(0, rows, grad_step, 0)
    for side, at, part in ((0, 0, 1), (1, cols - 1, 2)):
        beside = pl.ds(at, 1)
        u = halo_z[START, side] + res_r[None] * halo_z[RES, side] + img_r[None] * halo_z[IMG, side]
        v = res_a[None] * halo_z[COT, side] + img_a[None] * halo_z[ADJ, side]
        du = prob[1:rows + 1, beside, :] - u
        dv = adj[1:rows + 1, beside, :] - v
        grad[:, beside, :] = grad[:, beside, :] - rim_z[part, side] * (du * dv)
    copy = pltpu.make_async_copy(grad, grad_out, store_sem.at[2])
    copy.start()
    stores.append(copy)

    for k in range(6):
        for side in every:
            @pl.when(can_send[side])
            def _():
                exchange(k, side).wait_send()
    for k in range(1, n):
        share(k, me).wait_send()
    for copy in stores:
        copy.wait()


def per_device(ny, nz, conduct, seeds, labels, start, cotangent):
    rows, cols, lanes = conduct.shape
    n = ny * nz
    block = jax.ShapeDtypeStruct(conduct.shape, jnp.float32)
    f32 = jnp.float32
    return pl.pallas_call(
        functools.partial(kernel, ny, nz),
        out_shape=(block, block, block),
        in_specs=[pl.BlockSpec(memory_space=pl.ANY)] * 5,
        out_specs=[pl.BlockSpec(memory_space=pl.ANY)] * 3,
        scratch_shapes=[
            pltpu.VMEM((6, rows + 2, cols, lanes), f32),
            pltpu.VMEM((rows + 2, cols, lanes), f32),
            pltpu.VMEM((rows + 2, cols, lanes), f32),
            pltpu.VMEM((rows, cols, lanes), f32),
            pltpu.VMEM((rows, cols, lanes), jnp.int32),
            pltpu.VMEM((rows, cols, lanes), jnp.int32),
            pltpu.VMEM((3, rows + 1, cols, lanes), f32),
            pltpu.VMEM((3, rows, cols, lanes), f32),
            pltpu.VMEM((3, rows, cols, lanes), f32),
            pltpu.VMEM((3, 2, rows, 1, lanes), f32),
            pltpu.VMEM((6, 2, rows, 1, lanes), f32),
            pltpu.VMEM((6, 2, rows, 1, lanes), f32),
            pltpu.VMEM((n, 1, lanes), f32),
            pltpu.SemaphoreType.DMA((5,)),
            pltpu.SemaphoreType.DMA((3,)),
            pltpu.SemaphoreType.DMA((6, 4)),
            pltpu.SemaphoreType.DMA((6, 4)),
            pltpu.SemaphoreType.DMA((n,)),
            pltpu.SemaphoreType.DMA((n,)),
        ],
        compiler_params=pltpu.CompilerParams(collective_id=0, has_side_effects=True),
    )(conduct, seeds, labels, start, cotangent)


def solution(mesh):
    ny, nz = mesh.shape["gy"], mesh.shape["gz"]
    spec = P("gy", "gz", None)
    return jax.shard_map(
        functools.partial(per_device, ny, nz),
        mesh=mesh, in_specs=(spec,) * 5, out_specs=(spec,) * 3, check_vma=False,
    )
```

time: 205 us -> 31.7 us (0.15); the launches traced: 201 us -> 31.5 us
  blocking collectives: 87.9 us -> 0 us
  starting transfers between devices: 71.9 us -> 0 us
  Pallas kernels: 0 us -> 27.4 us
  waiting for transfers between devices: 16 us -> 0 us
  between operations: 13.2 us -> 0.65 us
  other arithmetic: 7.82 us -> 0 us
    psum x2 -> x0, blocking collectives: 87.9 us -> none  [paired_sums(): lax.psum((jnp.sum(resid * resid), jnp.sum(resid * image)), ('gy', 'gz'))]
    ppermute x28 -> x0, starting transfers between devices: 71.9 us -> none  [the longest x14 53.7 us: with_halo(): lax.ppermute(lax.slice_in_dim(block, block.shape[dim] - width, None, axis...]
    pallas_call x0 -> x1, Pallas kernels: none -> 27.4 us  [per_device(): pl.pallas_call(functools.partial(kernel, ny, nz), out_shape=(block, block...]
    ppermute x28 -> x0, waiting for transfers between devices: 16 us -> none  [the longest x14 14.7 us: with_halo(): lax.ppermute(lax.slice_in_dim(block, 0, width, axis=dim), axis, backward)]
    reduce_sum x6 -> x0, other arithmetic: 5.66 us -> none  [the longest x4 4.26 us: paired_sums(): jnp.sum(resid * image)]
    slice x11 -> x0, local copies, waits for them, and re-layouts: 2.93 us -> none  [the longest x5 2.25 us: with_halo(): lax.slice_in_dim(block, 0, width, axis=dim)]
    unnamed x20 -> x7, local copies, waits for them, and re-layouts: 1.11 us -> 3.46 us
  transfers between devices with their start and end apart: 28 -> 0, of which waited for: 8 -> 0; matrix products, arithmetic and copies ran while one was open for 3% -> 0% of each run, Pallas kernels for 0% -> 0%
where the time goes in v1:
time: 31.7 us; the launch traced here: 31.5 us
  Pallas kernels  27.4 us (86%)
  local copies, waits for them, and re-layouts  3.46 us (11%)
  between operations  0.65 us (2%)
    pallas_call x1, Pallas kernels, per_device(): pl.pallas_call(functools.partial(kernel, ny, nz), out_shape=(block, block...  27.4 us
    unnamed x7, local copies, waits for them, and re-layouts  3.46 us

profile of v1, /device:TPU:0, one launch (start us, length us, event | category | flops | bytes accessed | tf_op | source)
XLA Modules:
  0.0 31.5 jit_solution(14161753954654388766)
XLA Ops:
  0.6 27.4 %shard_map.76 = (f32[16,32,128]{2,1,0:T(8,128)}, f32[16,32,128]{2,1,0:T(8,128)}, f32[16,32,128]{2,1,0:T(8,128)}) custom-call(f32[16,32,128]{2,1,0:T(8,128)} %cond_in.1, s32[16,32,128]{2,1,0:T(8,128)} %seeds_in.1, s32[16,32,128]{2,1,0:T(8,128)} %labels_in.1, f32[16,32,128]{2,1,0:T(8,128)} %start_in.1, f32[16,32,128]{2,1,0:T(8,128)} %cot_in.1), custom_call_target="tpu_custom_call" | custom-call | tf_op jit(solution)/shard_map/pallas_call | solution.py:423
  28.1 0.0 copy-start.1
  28.1 1.7 %copy.11 = f32[16,32,128]{2,1,0:T(8,128)} copy(f32[16,32,128]{2,1,0:T(8,128)} %get-tuple-element.6) | data formatting | bytes 524288
  29.8 0.0 copy-done.1
  29.8 0.0 copy-start
  29.8 0.7 %copy.12 = f32[16,32,128]{2,1,0:T(8,128)} copy(f32[16,32,128]{2,1,0:T(8,128)S(1)} %copy-done.1) | data formatting | bytes 524288
  30.5 0.3 %copy-done = f32[16,32,128]{2,1,0:T(8,128)S(1)} copy-done((f32[16,32,128]{2,1,0:T(8,128)S(1)}, f32[16,32,128]{2,1,0:T(8,128)}, u32[]{:S(2)}) %copy-start) | copy-done | bytes 262168
  30.8 0.7 %copy.13 = f32[16,32,128]{2,1,0:T(8,128)} copy(f32[16,32,128]{2,1,0:T(8,128)S(1)} %copy-done) | data formatting | bytes 524288
Async XLA Ops:
  28.1 1.7 %copy-start.1 = (f32[16,32,128]{2,1,0:T(8,128)S(1)}, f32[16,32,128]{2,1,0:T(8,128)}, u32[]{:S(2)}) copy-start(f32[16,32,128]{2,1,0:T(8,128)} %get-tuple-element.7) | copy-start | bytes 786436
  29.8 1.0 %copy-start = (f32[16,32,128]{2,1,0:T(8,128)S(1)}, f32[16,32,128]{2,1,0:T(8,128)}, u32[]{:S(2)}) copy-start(f32[16,32,128]{2,1,0:T(8,128)} %get-tuple-element.8) | copy-start | bytes 786436

commit v2 on v1

--- a/solution.py
+++ b/solution.py
@@ -13,6 +13,25 @@
 MESH = pl.DeviceIdType.MESH
 COND, START, COT, RES, IMG, ADJ = range(6)
 LOW_Y, HIGH_Y, LOW_Z, HIGH_Z = range(4)
+
+
+UNROLL = 4
+
+
+def loop(low, high, step, carry):
+    whole = (high - low) // UNROLL
+
+    def block(i, carry):
+        for j in range(UNROLL):
+            carry = step(low + i * UNROLL + j, carry)
+        return carry
+
+    if whole > 1:
+        carry = lax.fori_loop(0, whole, block, carry)
+        low = low + whole * UNROLL
+    for y in range(low, high):
+        carry = step(y, carry)
+    return carry
 
 
 def kernel(
@@ -43,12 +62,19 @@
         copy.start()
         loads.append(copy)
 
+    def turn(position, step, size):
+        moved = position + step
+        return jnp.where(moved >= size, moved - size, moved)
+
+    def peer(k):
+        return turn(gy, k // nz, ny), turn(gz, k % nz, nz)
+
+    def slot_from(k):
+        return turn(gy, ny - k // nz, ny) * nz + turn(gz, nz - k % nz, nz)
+
     barrier = pltpu.get_barrier_semaphore()
     for k in range(1, n):
-        peer = lax.rem(me + k, n)
-        pl.semaphore_signal(
-            barrier, inc=1, device_id=(peer // nz, lax.rem(peer, nz)), device_id_type=MESH
-        )
+        pl.semaphore_signal(barrier, inc=1, device_id=peer(k), device_id_type=MESH)
 
     has_low_y, has_high_y = gy > 0, gy < ny - 1
     has_low_z, has_high_z = gz > 0, gz < nz - 1
@@ -160,8 +186,8 @@
         put_edge(edge_y, (y,), weigh(fields[COND, y], fields[COND, y + 1], None))
         return carry
 
-    lax.fori_loop(0, rows, edge_step, 0)
-    lax.fori_loop(1, rows, edge_y_step, 0)
+    loop(0, rows, edge_step, 0)
+    loop(1, rows, edge_y_step, 0)
     edge_y[0, 0] = plane
     edge_y[0, rows] = plane
     loads[2].wait()
@@ -186,7 +212,7 @@
             put(y, inner_plane(k, y))
             return carry
 
-        lax.fori_loop(1, rows - 1, step, 0)
+        loop(1, rows - 1, step, 0)
         put(rows - 1, inner_plane(k, rows - 1))
 
     def rim(k, out, sign):
@@ -253,7 +279,7 @@
             f = fields[k, y + 1]
             return norm + fold(f * f), product + fold(f * fields[out, y + 1])
 
-        norm, product = lax.fori_loop(0, rows, step, (zero8, zero8))
+        norm, product = loop(0, rows, step, (zero8, zero8))
         return total(product) / jnp.maximum(total(norm), 1e-30)
 
     def moments(k, out, shift):
@@ -279,7 +305,7 @@
             return tuple(c + fold(v) for c, v in zip(carry, [f2, fg, g2] + sums))
 
         first = step_first(k, out, shift, edge_sums)
-        return list(lax.fori_loop(1, rows, step, first))
+        return list(loop(1, rows, step, first))
 
     def step_first(k, out, shift, edge_sums):
         f = fields[k, 1]
@@ -328,10 +354,9 @@
     gathered[me] = jnp.sum(jnp.where(row16 == lane16, stack, 0.0), axis=0, keepdims=True)
 
     def share(k, slot):
-        peer = lax.rem(me + k, n)
         return pltpu.make_async_remote_copy(
             src_ref=gathered.at[slot], dst_ref=gathered.at[slot], send_sem=gsend_sem.at[k],
-            recv_sem=grecv_sem.at[k], device_id=(peer // nz, lax.rem(peer, nz)),
+            recv_sem=grecv_sem.at[k], device_id=peer(k),
             device_id_type=MESH,
         )
 
@@ -340,7 +365,7 @@
     arrive(IMG, (LOW_Y, LOW_Z))
     arrive(ADJ, (LOW_Y, LOW_Z))
     for k in range(1, n):
-        share(k, lax.rem(me + n - k, n)).wait_recv()
+        share(k, slot_from(k)).wait_recv()
 
     g = gathered[...].reshape(n, lanes)
 
@@ -373,7 +398,7 @@
         adj[y] = res_a * fields[COT, y] + img_a * fields[ADJ, y]
         return carry
 
-    lax.fori_loop(0, rows + 2, final_step, 0)
+    loop(0, rows + 2, final_step, 0)
     stores = [
         pltpu.make_async_copy(prob.at[body], prob_out, store_sem.at[0]),
         pltpu.make_async_copy(adj.at[body], adj_out, store_sem.at[1]),
@@ -392,7 +417,7 @@
         grad[y] = -out
         return carry
 
-    lax.fori_loop(0, rows, grad_step, 0)
+    loop(0, rows, grad_step, 0)
     for side, at, part in ((0, 0, 1), (1, cols - 1, 2)):
         beside = pl.ds(at, 1)
         u = halo_z[START, side] + res_r[None] * halo_z[RES, side] + img_r[None] * halo_z[IMG, side]

time: 31.7 us -> 27.8 us (0.88)
  Pallas kernels: 27.4 us -> 23.5 us
    pallas_call x1, Pallas kernels: 27.4 us -> 23.5 us  [per_device(): pl.pallas_call(functools.partial(kernel, ny, nz), out_shape=(block, block...]
where the time goes in v2:
time: 27.8 us; the launch traced here: 27.6 us
  Pallas kernels  23.5 us (85%)
  local copies, waits for them, and re-layouts  3.46 us (12%)
  between operations  0.65 us (2%)
    pallas_call x1, Pallas kernels, per_device(): pl.pallas_call(functools.partial(kernel, ny, nz), out_shape=(block, block...  23.5 us
    unnamed x7, local copies, waits for them, and re-layouts  3.46 us

profile of v2, /device:TPU:0, one launch (start us, length us, event | category | flops | bytes accessed | tf_op | source)
XLA Modules:
  0.0 27.6 jit_solution(6996272767169850913)
XLA Ops:
  0.6 23.5 %shard_map.76 = (f32[16,32,128]{2,1,0:T(8,128)}, f32[16,32,128]{2,1,0:T(8,128)}, f32[16,32,128]{2,1,0:T(8,128)}) custom-call(f32[16,32,128]{2,1,0:T(8,128)} %cond_in.1, s32[16,32,128]{2,1,0:T(8,128)} %seeds_in.1, s32[16,32,128]{2,1,0:T(8,128)} %labels_in.1, f32[16,32,128]{2,1,0:T(8,128)} %start_in.1, f32[16,32,128]{2,1,0:T(8,128)} %cot_in.1), custom_call_target="tpu_custom_call" | custom-call | tf_op jit(solution)/shard_map/pallas_call | solution.py:448
  24.1 0.0 copy-start.1
  24.1 1.7 %copy.11 = f32[16,32,128]{2,1,0:T(8,128)} copy(f32[16,32,128]{2,1,0:T(8,128)} %get-tuple-element.6) | data formatting | bytes 524288
  25.9 0.0 copy-done.1
  25.9 0.0 copy-start
  25.9 0.7 %copy.12 = f32[16,32,128]{2,1,0:T(8,128)} copy(f32[16,32,128]{2,1,0:T(8,128)S(1)} %copy-done.1) | data formatting | bytes 524288
  26.6 0.3 %copy-done = f32[16,32,128]{2,1,0:T(8,128)S(1)} copy-done((f32[16,32,128]{2,1,0:T(8,128)S(1)}, f32[16,32,128]{2,1,0:T(8,128)}, u32[]{:S(2)}) %copy-start) | copy-done | bytes 262168
  26.9 0.7 %copy.13 = f32[16,32,128]{2,1,0:T(8,128)} copy(f32[16,32,128]{2,1,0:T(8,128)S(1)} %copy-done) | data formatting | bytes 524288
Async XLA Ops:
  24.1 1.7 %copy-start.1 = (f32[16,32,128]{2,1,0:T(8,128)S(1)}, f32[16,32,128]{2,1,0:T(8,128)}, u32[]{:S(2)}) copy-start(f32[16,32,128]{2,1,0:T(8,128)} %get-tuple-element.7) | copy-start | bytes 786436
  25.9 1.0 %copy-start = (f32[16,32,128]{2,1,0:T(8,128)S(1)}, f32[16,32,128]{2,1,0:T(8,128)}, u32[]{:S(2)}) copy-start(f32[16,32,128]{2,1,0:T(8,128)} %get-tuple-element.8) | copy-start | bytes 786436

commit v3 on v2

--- a/solution.py
+++ b/solution.py
@@ -37,10 +37,10 @@
 def kernel(
     ny, nz,
     cond_in, seeds_in, labels_in, start_in, cot_in,
-    prob_out, adj_out, grad_out,
-    fields, prob, adj, grad, seeds, labels,
+    prob, adj, grad,
+    fields, seeds, labels,
     edge_y, edge_z, edge_x, rim_z, halo_z, face_z, gathered,
-    load_sem, store_sem, send_sem, recv_sem, gsend_sem, grecv_sem,
+    load_sem, send_sem, recv_sem, gsend_sem, grecv_sem,
 ):
     rows, cols, lanes = cond_in.shape
     n = ny * nz
@@ -256,14 +256,7 @@
     arrive(COT, every)
     rim(COT, ADJ, 1.0)
     put_faces(ADJ)
-
-    arrive(RES, every)
-    rim(RES, IMG, 1.0)
-    put_faces(IMG)
-    send(IMG, (HIGH_Y, HIGH_Z))
-    send(ADJ, (HIGH_Y, HIGH_Z))
-    send(IMG, (LOW_Y, LOW_Z))
-    send(ADJ, (LOW_Y, LOW_Z))
+    send(ADJ, every)
 
     def fold(value):
         return jnp.sum(value.reshape(cols // 8, 8, lanes), axis=0)
@@ -333,10 +326,16 @@
             ends.append(jnp.sum(a + b, axis=0, keepdims=True) + c)
         return [jnp.sum(v, axis=0, keepdims=True) for v in ends[:3]] + ends[3:]
 
+    shift_a = shift_of(COT, ADJ)
+    sums_a = moments(COT, ADJ, shift_a)
+    arrive(RES, every)
+    rim(RES, IMG, 1.0)
+    put_faces(IMG)
+    send(IMG, (HIGH_Y, HIGH_Z))
+    send(IMG, (LOW_Y, LOW_Z))
+
     shift_r = shift_of(RES, IMG)
     sums_r = moments(RES, IMG, shift_r)
-    shift_a = shift_of(COT, ADJ)
-    sums_a = moments(COT, ADJ, shift_a)
     arrive(ADJ, (HIGH_Y, HIGH_Z))
     sums_a = rim_moments(COT, ADJ, shift_a, sums_a)
     arrive(IMG, (HIGH_Y, HIGH_Z))
@@ -399,13 +398,6 @@
         return carry
 
     loop(0, rows + 2, final_step, 0)
-    stores = [
-        pltpu.make_async_copy(prob.at[body], prob_out, store_sem.at[0]),
-        pltpu.make_async_copy(adj.at[body], adj_out, store_sem.at[1]),
-    ]
-    for copy in stores:
-        copy.start()
-
     def grad_step(y, carry):
         u, v = prob[y + 1], adj[y + 1]
         d = (u - low_x(u)) * (v - low_x(v))
@@ -425,9 +417,6 @@
         du = prob[1:rows + 1, beside, :] - u
         dv = adj[1:rows + 1, beside, :] - v
         grad[:, beside, :] = grad[:, beside, :] - rim_z[part, side] * (du * dv)
-    copy = pltpu.make_async_copy(grad, grad_out, store_sem.at[2])
-    copy.start()
-    stores.append(copy)
 
     for k in range(6):
         for side in every:
@@ -436,7 +425,18 @@
                 exchange(k, side).wait_send()
     for k in range(1, n):
         share(k, me).wait_send()
-    for copy in stores:
+
+
+def put_out(prob, adj, grad, prob_out, adj_out, grad_out, sem):
+    body = pl.ds(1, grad.shape[0])
+    copies = [
+        pltpu.make_async_copy(prob.at[body], prob_out, sem.at[0]),
+        pltpu.make_async_copy(adj.at[body], adj_out, sem.at[1]),
+        pltpu.make_async_copy(grad, grad_out, sem.at[2]),
+    ]
+    for copy in copies:
+        copy.start()
+    for copy in copies:
         copy.wait()
 
 
@@ -445,16 +445,14 @@
     n = ny * nz
     block = jax.ShapeDtypeStruct(conduct.shape, jnp.float32)
     f32 = jnp.float32
-    return pl.pallas_call(
+    padded = pltpu.VMEM((rows + 2, cols, lanes), f32)
+    made = pl.pallas_call(
         functools.partial(kernel, ny, nz),
-        out_shape=(block, block, block),
+        out_shape=(padded, padded, pltpu.VMEM((rows, cols, lanes), f32)),
         in_specs=[pl.BlockSpec(memory_space=pl.ANY)] * 5,
-        out_specs=[pl.BlockSpec(memory_space=pl.ANY)] * 3,
+        out_specs=[pl.BlockSpec(memory_space=pltpu.VMEM)] * 3,
         scratch_shapes=[
             pltpu.VMEM((6, rows + 2, cols, lanes), f32),
-            pltpu.VMEM((rows + 2, cols, lanes), f32),
-            pltpu.VMEM((rows + 2, cols, lanes), f32),
-            pltpu.VMEM((rows, cols, lanes), f32),
             pltpu.VMEM((rows, cols, lanes), jnp.int32),
             pltpu.VMEM((rows, cols, lanes), jnp.int32),
             pltpu.VMEM((3, rows + 1, cols, lanes), f32),
@@ -465,7 +463,6 @@
             pltpu.VMEM((6, 2, rows, 1, lanes), f32),
             pltpu.VMEM((n, 1, lanes), f32),
             pltpu.SemaphoreType.DMA((5,)),
-            pltpu.SemaphoreType.DMA((3,)),
             pltpu.SemaphoreType.DMA((6, 4)),
             pltpu.SemaphoreType.DMA((6, 4)),
             pltpu.SemaphoreType.DMA((n,)),
@@ -473,6 +470,13 @@
         ],
         compiler_params=pltpu.CompilerParams(collective_id=0, has_side_effects=True),
     )(conduct, seeds, labels, start, cotangent)
+    return pl.pallas_call(
+        put_out,
+        out_shape=(block, block, block),
+        in_specs=[pl.BlockSpec(memory_space=pltpu.VMEM)] * 3,
+        out_specs=[pl.BlockSpec(memory_space=pl.ANY)] * 3,
+        scratch_shapes=[pltpu.SemaphoreType.DMA((3,))],
+    )(*made)
 
 
 def solution(mesh):

time: 27.8 us -> 27.6 us (level)
  local copies, waits for them, and re-layouts: 3.46 us -> 2.11 us
  Pallas kernels: 23.5 us -> 24.6 us
    unnamed x7 -> x6, local copies, waits for them, and re-layouts: 3.46 us -> 2.11 us
    pallas_call x1 -> x2, Pallas kernels: 23.5 us -> 24.6 us  [the longest x1 22.6 us: per_device(): pl.pallas_call(functools.partial(kernel, ny, nz), out_shape=(padded, padd...]
where the time goes in v3:
time: 27.6 us; the launch traced here: 27.4 us
  Pallas kernels  24.6 us (89%)
  local copies, waits for them, and re-layouts  2.11 us (8%)
  between operations  0.65 us (2%)
    pallas_call x1, Pallas kernels, per_device(): pl.pallas_call(functools.partial(kernel, ny, nz), out_shape=(padded, padd...  22.6 us
    unnamed x6, local copies, waits for them, and re-layouts  2.11 us
    pallas_call x1, Pallas kernels, per_device(): pl.pallas_call(put_out, out_shape=(block, block, block), in_specs=[pl.Blo...  2.03 us

profile of v3, /device:TPU:0, one launch (start us, length us, event | category | flops | bytes accessed | tf_op | source)
XLA Modules:
  0.0 27.4 jit_solution(8630953071459412230)
XLA Ops:
  0.6 22.6 %shard_map.76 = (f32[18,32,128]{2,1,0:T(8,128)S(1)}, f32[18,32,128]{2,1,0:T(8,128)S(1)}, f32[16,32,128]{2,1,0:T(8,128)S(1)}) custom-call(f32[16,32,128]{2,1,0:T(8,128)} %cond_in.1, s32[16,32,128]{2,1,0:T(8,128)} %seeds_in.1, s32[16,32,128]{2,1,0:T(8,128)} %labels_in.1, f32[16,32,128]{2,1,0:T(8,128)} %start_in.1, f32[16,32,128]{2,1,0:T(8,128)} %cot_in.1), custom_call_target="tpu_custom_call" | custom-call | tf_op jit(solution)/shard_map/pallas_call | solution.py:449
  23.3 0.0 copy-start
  23.3 0.7 %copy-done = f32[18,32,128]{2,1,0:T(8,128)} copy-done((f32[18,32,128]{2,1,0:T(8,128)}, f32[18,32,128]{2,1,0:T(8,128)S(1)}, u32[]{:S(2)}) %copy-start) | copy-done | bytes 294936
  24.0 0.0 copy-start.1
  24.0 0.7 %copy-done.1 = f32[18,32,128]{2,1,0:T(8,128)} copy-done((f32[18,32,128]{2,1,0:T(8,128)}, f32[18,32,128]{2,1,0:T(8,128)S(1)}, u32[]{:S(2)}) %copy-start.1) | copy-done | bytes 294936
  24.7 0.0 copy-start.2
  24.7 0.7 %copy-done.2 = f32[16,32,128]{2,1,0:T(8,128)} copy-done((f32[16,32,128]{2,1,0:T(8,128)}, f32[16,32,128]{2,1,0:T(8,128)S(1)}, u32[]{:S(2)}) %copy-start.2) | copy-done | bytes 262168
  25.4 2.0 %shard_map.77 = (f32[16,32,128]{2,1,0:T(8,128)}, f32[16,32,128]{2,1,0:T(8,128)}, f32[16,32,128]{2,1,0:T(8,128)}) custom-call(f32[18,32,128]{2,1,0:T(8,128)} %copy-done, f32[18,32,128]{2,1,0:T(8,128)} %copy-done.1, f32[16,32,128]{2,1,0:T(8,128)} %copy-done.2), custom_call_target="tpu_custom_call" | custom-call | tf_op jit(solution)/shard_map/pallas_call | solution.py:473
Async XLA Ops:
  23.3 0.7 %copy-start = (f32[18,32,128]{2,1,0:T(8,128)}, f32[18,32,128]{2,1,0:T(8,128)S(1)}, u32[]{:S(2)}) copy-start(f32[18,32,128]{2,1,0:T(8,128)S(1)} %get-tuple-element.6.prob) | copy-start | bytes 884740
  24.0 0.7 %copy-start.1 = (f32[18,32,128]{2,1,0:T(8,128)}, f32[18,32,128]{2,1,0:T(8,128)S(1)}, u32[]{:S(2)}) copy-start(f32[18,32,128]{2,1,0:T(8,128)S(1)} %get-tuple-element.7.adj) | copy-start | bytes 884740
  24.7 0.7 %copy-start.2 = (f32[16,32,128]{2,1,0:T(8,128)}, f32[16,32,128]{2,1,0:T(8,128)S(1)}, u32[]{:S(2)}) copy-start(f32[16,32,128]{2,1,0:T(8,128)S(1)} %get-tuple-element.8.grad) | copy-start | bytes 786436
